TPU v7x, 512 devices: a whole 4x8x8 slice. The times are simulated.
512 devices in a mesh: seq: 128 (over y, x_lo, z), ch: 4 (over x_hi, core).
Axes of the slice: x: 4 (x_hi: 2, x_lo: 2; x = x_hi * 2 + x_lo), y: 8, z: 8, core: 2. Of those that a mesh axis runs over, the one named last changes fastest.
Arguments:
- signal_x: bfloat16 [64, 65536], P('ch', 'seq'), may hold values from -6 to 6
- gate_q: bfloat16 [64, 65536], P('ch', 'seq'), may hold values from -6 to 6
- gate_k: bfloat16 [64, 65536], P('ch', 'seq'), may hold values from -6 to 6
- skip_gain: float32 [64], P('ch'), may hold values from 0.5 to 1.5
- residue: float32 [16], replicated, may hold values from -1.5 to 1.5
- memory: float32 [16], replicated, may hold values from 30 to 262144
- cotangent: bfloat16 [64, 65536], P('ch', 'seq'), may hold values from -6 to 6
Outputs:
- output: bfloat16 [64, 65536], P('ch', 'seq')
- grad_x: bfloat16 [64, 65536], P('ch', 'seq')
- grad_q: bfloat16 [64, 65536], P('ch', 'seq')
- grad_k: bfloat16 [64, 65536], P('ch', 'seq')
- grad_skip: float32 [64], P('ch')
- grad_residue: float32 [16], replicated
- grad_memory: float32 [16], replicated
All inputs are finite; a program needn't handle non-finite values.
Results may differ from a plain program's by a relative error of at most 0.002.
Values sent between devices are 32-bit elements; how exact they have to be, the bound alone decides.
A program may use at most 64 MiB of HBM per device.

v0:
```python
import math
import jax
import jax.numpy as jnp
from jax import lax
from jax.sharding import PartitionSpec as P

HIGH_PREC = lax.Precision.HIGHEST


def partner_2(shard, axis, stride):
    return lax.ppermute(shard, axis, [(i, i ^ 1 << stride) for i in range(lax.axis_size(axis))])


def cmul(left_op, right_op):
    return jnp.stack(
        [
            left_op[0] * right_op[0] - left_op[1] * right_op[1],
            left_op[0] * right_op[1] + left_op[1] * right_op[0],
        ]
    )


def dft_pair(order_len, orient):
    indices = jnp.arange(order_len, dtype=jnp.int32)
    products = indices[:, None] * indices[None, :] % order_len
    angles = products.astype(jnp.float32) * (2.0 * math.pi / order_len)
    return (jnp.cos(angles), orient * jnp.sin(angles))


def apply_matrix(signal_data, matrix_pair, pattern):
    with_cos = jnp.einsum(pattern, signal_data, matrix_pair[0], precision=HIGH_PREC)
    with_sin = jnp.einsum(pattern, signal_data, matrix_pair[1], precision=HIGH_PREC)
    return jnp.stack([with_cos[0] - with_sin[1], with_sin[0] + with_cos[1]])


def split_factor(local_len):
    chosen = 1
    factor = 1
    while factor * factor <= local_len:
        if local_len % factor == 0:
            chosen = factor
        factor = factor + 1
    return chosen


def inner_twiddle(outer_len, inner_len, orient):
    local_len = outer_len * inner_len
    rows_idx = jnp.arange(outer_len, dtype=jnp.int32)
    cols_idx = jnp.arange(inner_len, dtype=jnp.int32)
    products = rows_idx[:, None] * cols_idx[None, :] % local_len
    angles = products.astype(jnp.float32) * (2.0 * math.pi / local_len)
    return jnp.stack([jnp.cos(angles), orient * jnp.sin(angles)])[:, None, None]


def local_forward(signal_data):
    local_len = signal_data.shape[-1]
    outer_len = split_factor(local_len)
    inner_len = local_len // outer_len
    shaped = signal_data.reshape(signal_data.shape[:3] + (outer_len, inner_len))
    shaped = apply_matrix(shaped, dft_pair(outer_len, -1.0), "zsxab,ak->zsxkb")
    shaped = cmul(shaped, inner_twiddle(outer_len, inner_len, -1.0))
    shaped = apply_matrix(shaped, dft_pair(inner_len, -1.0), "zsxkb,bc->zsxkc")
    return shaped.reshape(signal_data.shape)


def local_inverse(signal_data):
    local_len = signal_data.shape[-1]
    outer_len = split_factor(local_len)
    inner_len = local_len // outer_len
    shaped = signal_data.reshape(signal_data.shape[:3] + (outer_len, inner_len))
    shaped = apply_matrix(shaped, dft_pair(inner_len, 1.0), "zsxkc,cb->zsxkb")
    shaped = cmul(shaped, inner_twiddle(outer_len, inner_len, 1.0))
    shaped = apply_matrix(shaped, dft_pair(outer_len, 1.0), "zsxkb,kj->zsxjb")
    return shaped.reshape(signal_data.shape)


def global_twiddle(freq_block, local_len, full_len, orient):
    slot_ids = jnp.arange(2, dtype=jnp.int32)
    freq_ids = 2 * freq_block + slot_ids
    products = freq_ids[:, None] * jnp.arange(local_len, dtype=jnp.int32)[None, :]
    angles = products.astype(jnp.float32) * (2.0 * math.pi / full_len)
    return jnp.stack([jnp.cos(angles), orient * jnp.sin(angles)])[:, None]


def bit_reverse(seq_index, sections):
    reversed_idx = jnp.zeros((), jnp.int32)
    for bit_level in range(sections):
        reversed_idx = reversed_idx | (seq_index >> bit_level & 1) << sections - 1 - bit_level
    return reversed_idx


def level_weight(seq_index, bit_level, orient):
    offset = seq_index & (1 << bit_level) - 1
    angles = offset.astype(jnp.float32) * (2.0 * math.pi / 2 ** (bit_level + 1))
    is_upper = seq_index >> bit_level & 1
    return (jnp.stack([jnp.cos(angles), orient * jnp.sin(angles)]), is_upper)


def forward_partners(signal_data, sections):
    seq_index = lax.axis_index("seq")
    for bit_level in range(sections - 1, -1, -1):
        partner = partner_2(signal_data, "seq", bit_level)
        weight, is_upper = level_weight(seq_index, bit_level, -1.0)
        summed = signal_data + partner
        differ = cmul(partner - signal_data, weight)
        signal_data = jnp.where(is_upper == 1, differ, summed)
    return signal_data


def inverse_partners(signal_data, sections):
    seq_index = lax.axis_index("seq")
    for bit_level in range(sections):
        partner = partner_2(signal_data, "seq", bit_level)
        weight, is_upper = level_weight(seq_index, bit_level, 1.0)
        lower_new = signal_data + cmul(partner, weight)
        upper_new = partner - cmul(signal_data, weight)
        signal_data = jnp.where(is_upper == 1, upper_new, lower_new)
    return signal_data


def forward_transform(signals, sections):
    seq_index = lax.axis_index("seq")
    devices = lax.axis_size("seq")
    local_len = signals.shape[-1]
    full_len = 2 * devices * local_len
    angles = seq_index.astype(jnp.float32) * (math.pi / devices)
    weight = jnp.stack([jnp.cos(angles), -jnp.sin(angles)])
    signal_data = jnp.stack([signals, cmul(signals, weight)], axis=2)
    signal_data = forward_partners(signal_data, sections)
    freq_block = bit_reverse(seq_index, sections)
    signal_data = cmul(signal_data, global_twiddle(freq_block, local_len, full_len, -1.0))
    return local_forward(signal_data)


def inverse_transform(spectra, sections):
    seq_index = lax.axis_index("seq")
    devices = lax.axis_size("seq")
    local_len = spectra.shape[-1]
    full_len = 2 * devices * local_len
    signal_data = local_inverse(spectra)
    freq_block = bit_reverse(seq_index, sections)
    signal_data = cmul(signal_data, global_twiddle(freq_block, local_len, full_len, 1.0))
    signal_data = inverse_partners(signal_data, sections)
    angles = seq_index.astype(jnp.float32) * (math.pi / devices)
    weight = jnp.stack([jnp.cos(angles), jnp.sin(angles)])
    result = signal_data[:, :, 0] + cmul(signal_data[:, :, 1], weight)
    return result / full_len


def per_device(signal_x, gate_q, gate_k, skip_gain, residue, memory, cotangent):
    channels, local_len = signal_x.shape
    devices = lax.axis_size("seq")
    sections = devices.bit_length() - 1
    seq_index = lax.axis_index("seq")
    positions = (seq_index * local_len + jnp.arange(local_len, dtype=jnp.int32)).astype(jnp.float32)
    weights = jnp.sqrt(2.0 / memory)[:, None] * jnp.exp(-positions[None, :] / memory[:, None])
    filter_taps = jnp.sum(residue[:, None] * weights, axis=0)
    x_float = signal_x.astype(jnp.float32)
    q_float = gate_q.astype(jnp.float32)
    k_float = gate_k.astype(jnp.float32)
    d_float = cotangent.astype(jnp.float32)
    values = x_float * k_float
    grad_mixed = d_float * q_float
    value_sig = jnp.stack([values, jnp.zeros_like(values)])
    grad_sig = jnp.stack([grad_mixed, jnp.zeros_like(grad_mixed)])
    sig_count = value_sig.shape[1]
    taps_sig = jnp.stack([filter_taps, jnp.zeros_like(filter_taps)])[:, None]
    spectra = forward_transform(jnp.concatenate([value_sig, taps_sig], axis=1), sections)
    value_spec = spectra[:, :sig_count]
    taps_spec = spectra[:, sig_count:]
    conv_sig = inverse_transform(cmul(value_spec, taps_spec), sections)
    grad_spec = forward_transform(grad_sig, sections)
    conj_sign = jnp.array([1.0, -1.0], jnp.float32).reshape(2, 1, 1, 1)
    back_spec = cmul(taps_spec * conj_sign, grad_spec)
    cross_spec = jnp.sum(cmul(value_spec * conj_sign, grad_spec), axis=1, keepdims=True)
    back_sig = inverse_transform(jnp.concatenate([back_spec, cross_spec], axis=1), sections)
    grad_taps = back_sig[0, sig_count]
    conv_out = conv_sig[0]
    corr_out = back_sig[0, :sig_count]
    mixed_out = conv_out + skip_gain[:, None] * values
    output = (q_float * mixed_out).astype(jnp.bfloat16)
    grad_values = skip_gain[:, None] * grad_mixed + corr_out
    grad_x = (grad_values * k_float).astype(jnp.bfloat16)
    grad_q = (d_float * mixed_out).astype(jnp.bfloat16)
    grad_k = (grad_values * x_float).astype(jnp.bfloat16)
    weighted = weights * grad_taps[None, :]
    part_residue = jnp.sum(weighted, axis=1)
    part_memory = residue * jnp.sum(weighted * (positions[None, :] / memory[:, None] - 0.5), axis=1)
    part_skip = jnp.sum(grad_mixed * values, axis=1)
    all_channels = channels * lax.axis_size("ch")
    seq_total = devices * local_len
    sum_residue, sum_memory = lax.psum((part_residue, part_memory), ("seq", "ch"))
    sum_skip = lax.psum(part_skip, "seq")
    norm_scale = 1.0 / math.sqrt(all_channels * seq_total)
    grad_skip = sum_skip / math.sqrt(seq_total)
    grad_residue = sum_residue * norm_scale
    grad_memory = sum_memory * norm_scale
    return (output, grad_x, grad_q, grad_k, grad_skip, grad_residue, grad_memory)


def solution(mesh):
    return jax.shard_map(
        per_device,
        mesh=mesh,
        in_specs=(
            P("ch", "seq"),
            P("ch", "seq"),
            P("ch", "seq"),
            P("ch"),
            P(),
            P(),
            P("ch", "seq"),
        ),
        out_specs=(
            P("ch", "seq"),
            P("ch", "seq"),
            P("ch", "seq"),
            P("ch", "seq"),
            P("ch"),
            P(),
            P(),
        ),
        check_vma=False,
    )
```

profile of v0, /device:TPU:4, one launch (start us, length us, event | category | flops | bytes accessed | tf_op | source)
XLA Modules:
  0.0 616.5 jit_solution(16483242981298394517)
XLA Ops:
  0.8 0.6 copy-done.6
  2.3 7.7 %collective-permute-start = (f32[2,17,2,512]{3,1,2,0:T(8,128)S(1)}, f32[2,17,2,512]{3,1,2,0:T(8,128)S(1)}, u32[]{:S(2)}, u32[]{:S(2)}) collective-permute-start(f32[2,17,2,512]{3,1,2,0:T(8,128)S(1)} %pad_maximum_fusion.13), channel_id=1, source_target_pairs={{0,256},{4,260},{8,264},{12,268},{16,272},{20,276},{24,280},{28,28... | collective-permute-start | bytes 417800 | tf_op jit(solution)/shard_map/ppermute | solution.py:11
  10.1 2.0 collective-permute-start.14
  13.4 10.8 %collective-permute-done.14 = f32[2,16,2,512]{3,1,0,2:T(8,128)S(1)} collective-permute-done((f32[2,16,2,512]{3,1,0,2:T(8,128)S(1)}, f32[2,16,2,512]{3,1,0,2:T(8,128)S(1)}, u32[]{:S(2)}, u32[]{:S(2)}) %collective-permute-start.14) | collective-permute-done | bytes 131104 | tf_op jit(solution)/shard_map/ppermute | solution.py:11
  24.4 4.9 collective-permute-start.15
  29.4 1.9 collective-permute-start.1
  31.4 7.9 %collective-permute-done.15 = f32[2,16,2,512]{3,1,0,2:T(8,128)S(1)} collective-permute-done((f32[2,16,2,512]{3,1,0,2:T(8,128)S(1)}, f32[2,16,2,512]{3,1,0,2:T(8,128)S(1)}, u32[]{:S(2)}, u32[]{:S(2)}) %collective-permute-start.15) | collective-permute-done | bytes 131104 | tf_op jit(solution)/shard_map/ppermute | solution.py:11
  39.4 1.9 collective-permute-start.16
  41.3 1.8 collective-permute-done.1
  43.3 2.1 collective-permute-start.2
  45.5 0.8 collective-permute-done.16
  46.3 3.1 collective-permute-start.17
  49.4 2.4 collective-permute-done.2
  51.9 3.1 collective-permute-start.3
  55.1 10.9 %collective-permute-start.18 = (f32[2,16,2,512]{3,1,0,2:T(8,128)S(1)}, f32[2,16,2,512]{3,1,0,2:T(8,128)S(1)}, u32[]{:S(2)}, u32[]{:S(2)}) collective-permute-start(f32[2,16,2,512]{3,1,0,2:T(8,128)S(1)} %maximum_select_fusion.10), channel_id=1, source_target_pairs={{0,16},{4,20},{8,24},{12,28},{16,0},{20,4},{24,8},{28,12},{32,48},... | collective-permute-start | bytes 393224 | tf_op jit(solution)/shard_map/ppermute | solution.py:11
  66.2 4.3 collective-permute-start.4
  70.8 7.4 %collective-permute-start.19 = (f32[2,16,2,512]{3,1,0,2:T(8,128)S(1)}, f32[2,16,2,512]{3,1,0,2:T(8,128)S(1)}, u32[]{:S(2)}, u32[]{:S(2)}) collective-permute-start(f32[2,16,2,512]{3,1,0,2:T(8,128)S(1)} %maximum_select_fusion.11), channel_id=1, source_target_pairs={{0,8},{4,12},{8,0},{12,4},{16,24},{20,28},{24,16},{28,20},{32,40},... | collective-permute-start | bytes 393224 | tf_op jit(solution)/shard_map/ppermute | solution.py:11
  78.2 3.5 collective-permute-done.4
  81.8 4.0 collective-permute-start.5
  85.8 3.4 collective-permute-done.19
  89.3 2.0 collective-permute-start.20
  91.3 4.3 collective-permute-done.5
  95.7 2.1 collective-permute-start.6
  98.9 0.6 convolution_bitcast_fusion.4
  99.5 0.6 convolution_bitcast_fusion.5
  100.1 4.2 collective-permute-done.6
  105.0 0.6 convolution_bitcast_fusion.2
  105.6 0.6 convolution_bitcast_fusion.3
  106.4 1.1 fusion
  107.5 1.1 fusion.2
  109.6 0.6 fusion.46
  110.2 0.6 fusion.52
  111.1 0.6 fusion.4
  111.7 0.6 fusion.5
  112.4 0.6 copy-done.4
  114.1 0.7 fusion.7
  114.8 0.7 fusion.6
  115.6 0.9 convolution_bitcast_fusion.1
  116.5 0.6 convolution_bitcast_fusion
  118.9 2.2 collective-permute-start.21
  121.6 3.6 collective-permute-start.7
  125.2 4.2 collective-permute-done.7
  129.5 2.8 collective-permute-start.8
  132.5 3.9 collective-permute-start.22
  136.4 9.4 %collective-permute-done.8 = f32[2,16,2,512]{3,1,0,2:T(8,128)S(1)} collective-permute-done((f32[2,16,2,512]{3,1,0,2:T(8,128)S(1)}, f32[2,16,2,512]{3,1,0,2:T(8,128)S(1)}, u32[]{:S(2)}, u32[]{:S(2)}) %collective-permute-start.8) | collective-permute-done | bytes 131104 | tf_op jit(solution)/shard_map/ppermute | solution.py:11
  145.9 4.5 collective-permute-start.9
  150.6 5.6 collective-permute-start.23
  156.3 1.6 collective-permute-done.9
  157.9 7.1 %collective-permute-start.10 = (f32[2,16,2,512]{3,1,0,2:T(8,128)S(1)}, f32[2,16,2,512]{3,1,0,2:T(8,128)S(1)}, u32[]{:S(2)}, u32[]{:S(2)}) collective-permute-start(f32[2,16,2,512]{3,1,0,2:T(8,128)S(1)} %fusion.17), channel_id=1, source_target_pairs={{0,32},{4,36},{8,40},{12,44},{16,48},{20,52},{24,56},{28,60},{32,0... | collective-permute-start | bytes 393224 | tf_op jit(solution)/shard_map/ppermute | solution.py:11
  165.1 0.7 collective-permute-done.23
  165.9 3.3 collective-permute-start.24
  169.3 3.7 collective-permute-start.11
  173.6 3.3 collective-permute-start.25
  177.0 4.4 collective-permute-start.12
  181.9 4.4 collective-permute-start.26
  186.4 2.8 collective-permute-done.12
  189.2 4.3 collective-permute-start.13
  193.5 4.0 collective-permute-done.26
  197.6 4.7 collective-permute-start.27
  202.5 10.7 %collective-permute-done.27 = f32[2,17,2,512]{3,1,2,0:T(8,128)S(1)} collective-permute-done((f32[2,17,2,512]{3,1,2,0:T(8,128)S(1)}, f32[2,17,2,512]{3,1,2,0:T(8,128)S(1)}, u32[]{:S(2)}, u32[]{:S(2)}) %collective-permute-start.27) | collective-permute-done | bytes 139296 | tf_op jit(solution)/shard_map/ppermute | solution.py:11
  213.6 93.2 %all-reduce.3 = (f32[16]{0:T(128)S(1)}, f32[16]{0:T(128)S(1)}) all-reduce(f32[16]{0:T(128)S(1)} %get-tuple-element.8, f32[16]{0:T(128)S(1)} %mul.2458), channel_id=1, replica_groups=mesh['seq'=128,'ch'=4] {'seq','ch'}, use_global_device_ids=true, to_apply=%region_5.6 | all-reduce | flops 32 | bytes 256 | tf_op jit(solution)/shard_map/psum | solution.py:192
  307.9 0.8 fusion.29
  308.7 0.6 fusion.28
  309.3 306.7 %psum.21 = f32[16]{0:T(128)S(1)} all-reduce(f32[16]{0:T(128)S(1)} %get-tuple-element.130), channel_id=1, replica_groups=mesh['seq'=128,'ch'=4] {'seq'}, use_global_device_ids=true, to_apply=%region_3.4 | all-reduce | flops 16 | bytes 128 | tf_op jit(solution)/shard_map/psum | solution.py:193
  (195 shorter events, 12.9 us)
Async XLA Ops:
  0.8 0.7 copy-start.6
  0.8 0.7 copy-start.7
  1.4 0.7 copy-start.2
  1.5 0.7 copy-start.1
  2.3 7.8 %copy-start = (bf16[16,512]{1,0:T(8,128)(2,1)S(1)}, bf16[16,512]{1,0:T(8,128)(2,1)}, u32[]{:S(2)}) copy-start(bf16[16,512]{1,0:T(8,128)(2,1)} %param.9) | copy-start | bytes 49156
  2.3 7.8 %copy-start.3 = (bf16[16,512]{1,0:T(8,128)(2,1)S(1)}, bf16[16,512]{1,0:T(8,128)(2,1)}, u32[]{:S(2)}) copy-start(bf16[16,512]{1,0:T(8,128)(2,1)} %param.14) | copy-start | bytes 49156
  2.3 27.0 %collective-permute-start = (f32[2,17,2,512]{3,1,2,0:T(8,128)S(1)}, f32[2,17,2,512]{3,1,2,0:T(8,128)S(1)}, u32[]{:S(2)}, u32[]{:S(2)}) collective-permute-start(f32[2,17,2,512]{3,1,2,0:T(8,128)S(1)} %pad_maximum_fusion.13), channel_id=1, source_target_pairs={{0,256},{4,260},{8,264},{12,268},{16,272},{20,276},{24,280},{28,28... | collective-permute-start | bytes 417800 | tf_op jit(solution)/shard_map/ppermute | solution.py:11
  10.1 14.1 %collective-permute-start.14 = (f32[2,16,2,512]{3,1,0,2:T(8,128)S(1)}, f32[2,16,2,512]{3,1,0,2:T(8,128)S(1)}, u32[]{:S(2)}, u32[]{:S(2)}) collective-permute-start(f32[2,16,2,512]{3,1,0,2:T(8,128)S(1)} %pad_maximum_fusion.16), channel_id=1, source_target_pairs={{0,256},{4,260},{8,264},{12,268},{16,272},{20,276},{24,280},{28,28... | collective-permute-start | bytes 393224 | tf_op jit(solution)/shard_map/ppermute | solution.py:11
  24.4 14.9 %collective-permute-start.15 = (f32[2,16,2,512]{3,1,0,2:T(8,128)S(1)}, f32[2,16,2,512]{3,1,0,2:T(8,128)S(1)}, u32[]{:S(2)}, u32[]{:S(2)}) collective-permute-start(f32[2,16,2,512]{3,1,0,2:T(8,128)S(1)} %maximum_select_fusion.7), channel_id=1, source_target_pairs={{0,128},{4,132},{8,136},{12,140},{16,144},{20,148},{24,152},{28,15... | collective-permute-start | bytes 393224 | tf_op jit(solution)/shard_map/ppermute | solution.py:11
  29.4 13.7 %collective-permute-start.1 = (f32[2,17,2,512]{3,1,2,0:T(8,128)S(1)}, f32[2,17,2,512]{3,1,2,0:T(8,128)S(1)}, u32[]{:S(2)}, u32[]{:S(2)}) collective-permute-start(f32[2,17,2,512]{3,1,2,0:T(8,128)S(1)} %maximum_select_fusion), channel_id=1, source_target_pairs={{0,128},{4,132},{8,136},{12,140},{16,144},{20,148},{24,152},{28,15... | collective-permute-start | bytes 417800 | tf_op jit(solution)/shard_map/ppermute | solution.py:11
  39.4 6.9 %collective-permute-start.16 = (f32[2,16,2,512]{3,1,0,2:T(8,128)S(1)}, f32[2,16,2,512]{3,1,0,2:T(8,128)S(1)}, u32[]{:S(2)}, u32[]{:S(2)}) collective-permute-start(f32[2,16,2,512]{3,1,0,2:T(8,128)S(1)} %maximum_select_fusion.8), channel_id=1, source_target_pairs={{0,64},{4,68},{8,72},{12,76},{16,80},{20,84},{24,88},{28,92},{32,9... | collective-permute-start | bytes 393224 | tf_op jit(solution)/shard_map/ppermute | solution.py:11
  43.3 8.5 %collective-permute-start.2 = (f32[2,17,2,512]{3,1,2,0:T(8,128)S(1)}, f32[2,17,2,512]{3,1,2,0:T(8,128)S(1)}, u32[]{:S(2)}, u32[]{:S(2)}) collective-permute-start(f32[2,17,2,512]{3,1,2,0:T(8,128)S(1)} %maximum_select_fusion.1), channel_id=1, source_target_pairs={{0,64},{4,68},{8,72},{12,76},{16,80},{20,84},{24,88},{28,92},{32,9... | collective-permute-start | bytes 417800 | tf_op jit(solution)/shard_map/ppermute | solution.py:11
  46.3 8.7 %collective-permute-start.17 = (f32[2,16,2,512]{3,1,0,2:T(8,128)S(1)}, f32[2,16,2,512]{3,1,0,2:T(8,128)S(1)}, u32[]{:S(2)}, u32[]{:S(2)}) collective-permute-start(f32[2,16,2,512]{3,1,0,2:T(8,128)S(1)} %maximum_select_fusion.9), channel_id=1, source_target_pairs={{0,32},{4,36},{8,40},{12,44},{16,48},{20,52},{24,56},{28,60},{32,0... | collective-permute-start | bytes 393224 | tf_op jit(solution)/shard_map/ppermute | solution.py:11
  51.9 14.1 %collective-permute-start.3 = (f32[2,17,2,512]{3,1,2,0:T(8,128)S(1)}, f32[2,17,2,512]{3,1,2,0:T(8,128)S(1)}, u32[]{:S(2)}, u32[]{:S(2)}) collective-permute-start(f32[2,17,2,512]{3,1,2,0:T(8,128)S(1)} %maximum_select_fusion.2), channel_id=1, source_target_pairs={{0,32},{4,36},{8,40},{12,44},{16,48},{20,52},{24,56},{28,60},{32,0... | collective-permute-start | bytes 417800 | tf_op jit(solution)/shard_map/ppermute | solution.py:11
  55.1 15.6 %collective-permute-start.18 = (f32[2,16,2,512]{3,1,0,2:T(8,128)S(1)}, f32[2,16,2,512]{3,1,0,2:T(8,128)S(1)}, u32[]{:S(2)}, u32[]{:S(2)}) collective-permute-start(f32[2,16,2,512]{3,1,0,2:T(8,128)S(1)} %maximum_select_fusion.10), channel_id=1, source_target_pairs={{0,16},{4,20},{8,24},{12,28},{16,0},{20,4},{24,8},{28,12},{32,48},... | collective-permute-start | bytes 393224 | tf_op jit(solution)/shard_map/ppermute | solution.py:11
  66.2 15.5 %collective-permute-start.4 = (f32[2,17,2,512]{3,1,2,0:T(8,128)S(1)}, f32[2,17,2,512]{3,1,2,0:T(8,128)S(1)}, u32[]{:S(2)}, u32[]{:S(2)}) collective-permute-start(f32[2,17,2,512]{3,1,2,0:T(8,128)S(1)} %maximum_select_fusion.3), channel_id=1, source_target_pairs={{0,16},{4,20},{8,24},{12,28},{16,0},{20,4},{24,8},{28,12},{32,48},... | collective-permute-start | bytes 417800 | tf_op jit(solution)/shard_map/ppermute | solution.py:11
  70.8 18.4 %collective-permute-start.19 = (f32[2,16,2,512]{3,1,0,2:T(8,128)S(1)}, f32[2,16,2,512]{3,1,0,2:T(8,128)S(1)}, u32[]{:S(2)}, u32[]{:S(2)}) collective-permute-start(f32[2,16,2,512]{3,1,0,2:T(8,128)S(1)} %maximum_select_fusion.11), channel_id=1, source_target_pairs={{0,8},{4,12},{8,0},{12,4},{16,24},{20,28},{24,16},{28,20},{32,40},... | collective-permute-start | bytes 393224 | tf_op jit(solution)/shard_map/ppermute | solution.py:11
  81.8 13.8 %collective-permute-start.5 = (f32[2,17,2,512]{3,1,2,0:T(8,128)S(1)}, f32[2,17,2,512]{3,1,2,0:T(8,128)S(1)}, u32[]{:S(2)}, u32[]{:S(2)}) collective-permute-start(f32[2,17,2,512]{3,1,2,0:T(8,128)S(1)} %maximum_select_fusion.4), channel_id=1, source_target_pairs={{0,8},{4,12},{8,0},{12,4},{16,24},{20,28},{24,16},{28,20},{32,40},... | collective-permute-start | bytes 417800 | tf_op jit(solution)/shard_map/ppermute | solution.py:11
  89.3 8.9 %collective-permute-start.20 = (f32[2,16,2,512]{3,1,0,2:T(8,128)S(1)}, f32[2,16,2,512]{3,1,0,2:T(8,128)S(1)}, u32[]{:S(2)}, u32[]{:S(2)}) collective-permute-start(f32[2,16,2,512]{3,1,0,2:T(8,128)S(1)} %maximum_select_fusion.12), channel_id=1, source_target_pairs={{0,4},{4,0},{8,12},{12,8},{16,20},{20,16},{24,28},{28,24},{32,36},... | collective-permute-start | bytes 393224 | tf_op jit(solution)/shard_map/ppermute | solution.py:11
  95.7 8.6 %collective-permute-start.6 = (f32[2,17,2,512]{3,1,2,0:T(8,128)S(1)}, f32[2,17,2,512]{3,1,2,0:T(8,128)S(1)}, u32[]{:S(2)}, u32[]{:S(2)}) collective-permute-start(f32[2,17,2,512]{3,1,2,0:T(8,128)S(1)} %maximum_select_fusion.5), channel_id=1, source_target_pairs={{0,4},{4,0},{8,12},{12,8},{16,20},{20,16},{24,28},{28,24},{32,36},... | collective-permute-start | bytes 417800 | tf_op jit(solution)/shard_map/ppermute | solution.py:11
  112.4 0.7 copy-start.4
  118.9 13.5 %collective-permute-start.21 = (f32[2,17,2,512]{3,1,2,0:T(8,128)S(1)}, f32[2,17,2,512]{3,1,2,0:T(8,128)S(1)}, u32[]{:S(2)}, u32[]{:S(2)}) collective-permute-start(f32[2,17,2,512]{3,1,2,0:T(8,128)S(1)} %pad_maximum_fusion.14), channel_id=1, source_target_pairs={{0,4},{4,0},{8,12},{12,8},{16,20},{20,16},{24,28},{28,24},{32,36},... | collective-permute-start | bytes 417800 | tf_op jit(solution)/shard_map/ppermute | solution.py:11
  121.6 7.9 %collective-permute-start.7 = (f32[2,16,2,512]{3,1,0,2:T(8,128)S(1)}, f32[2,16,2,512]{3,1,0,2:T(8,128)S(1)}, u32[]{:S(2)}, u32[]{:S(2)}) collective-permute-start(f32[2,16,2,512]{3,1,0,2:T(8,128)S(1)} %pad_maximum_fusion.15), channel_id=1, source_target_pairs={{0,4},{4,0},{8,12},{12,8},{16,20},{20,16},{24,28},{28,24},{32,36},... | collective-permute-start | bytes 393224 | tf_op jit(solution)/shard_map/ppermute | solution.py:11
  129.5 16.3 %collective-permute-start.8 = (f32[2,16,2,512]{3,1,0,2:T(8,128)S(1)}, f32[2,16,2,512]{3,1,0,2:T(8,128)S(1)}, u32[]{:S(2)}, u32[]{:S(2)}) collective-permute-start(f32[2,16,2,512]{3,1,0,2:T(8,128)S(1)} %fusion.15), channel_id=1, source_target_pairs={{0,8},{4,12},{8,0},{12,4},{16,24},{20,28},{24,16},{28,20},{32,40},... | collective-permute-start | bytes 393224 | tf_op jit(solution)/shard_map/ppermute | solution.py:11
  132.5 17.9 %collective-permute-start.22 = (f32[2,17,2,512]{3,1,2,0:T(8,128)S(1)}, f32[2,17,2,512]{3,1,2,0:T(8,128)S(1)}, u32[]{:S(2)}, u32[]{:S(2)}) collective-permute-start(f32[2,17,2,512]{3,1,2,0:T(8,128)S(1)} %fusion.8), channel_id=1, source_target_pairs={{0,8},{4,12},{8,0},{12,4},{16,24},{20,28},{24,16},{28,20},{32,40},... | collective-permute-start | bytes 417800 | tf_op jit(solution)/shard_map/ppermute | solution.py:11
  145.9 11.9 %collective-permute-start.9 = (f32[2,16,2,512]{3,1,0,2:T(8,128)S(1)}, f32[2,16,2,512]{3,1,0,2:T(8,128)S(1)}, u32[]{:S(2)}, u32[]{:S(2)}) collective-permute-start(f32[2,16,2,512]{3,1,0,2:T(8,128)S(1)} %fusion.16), channel_id=1, source_target_pairs={{0,16},{4,20},{8,24},{12,28},{16,0},{20,4},{24,8},{28,12},{32,48},... | collective-permute-start | bytes 393224 | tf_op jit(solution)/shard_map/ppermute | solution.py:11
  150.6 15.2 %collective-permute-start.23 = (f32[2,17,2,512]{3,1,2,0:T(8,128)S(1)}, f32[2,17,2,512]{3,1,2,0:T(8,128)S(1)}, u32[]{:S(2)}, u32[]{:S(2)}) collective-permute-start(f32[2,17,2,512]{3,1,2,0:T(8,128)S(1)} %fusion.9), channel_id=1, source_target_pairs={{0,16},{4,20},{8,24},{12,28},{16,0},{20,4},{24,8},{28,12},{32,48},... | collective-permute-start | bytes 417800 | tf_op jit(solution)/shard_map/ppermute | solution.py:11
  157.9 11.3 %collective-permute-start.10 = (f32[2,16,2,512]{3,1,0,2:T(8,128)S(1)}, f32[2,16,2,512]{3,1,0,2:T(8,128)S(1)}, u32[]{:S(2)}, u32[]{:S(2)}) collective-permute-start(f32[2,16,2,512]{3,1,0,2:T(8,128)S(1)} %fusion.17), channel_id=1, source_target_pairs={{0,32},{4,36},{8,40},{12,44},{16,48},{20,52},{24,56},{28,60},{32,0... | collective-permute-start | bytes 393224 | tf_op jit(solution)/shard_map/ppermute | solution.py:11
  165.9 7.6 %collective-permute-start.24 = (f32[2,17,2,512]{3,1,2,0:T(8,128)S(1)}, f32[2,17,2,512]{3,1,2,0:T(8,128)S(1)}, u32[]{:S(2)}, u32[]{:S(2)}) collective-permute-start(f32[2,17,2,512]{3,1,2,0:T(8,128)S(1)} %fusion.10), channel_id=1, source_target_pairs={{0,32},{4,36},{8,40},{12,44},{16,48},{20,52},{24,56},{28,60},{32,0... | collective-permute-start | bytes 417800 | tf_op jit(solution)/shard_map/ppermute | solution.py:11
  169.3 7.6 %collective-permute-start.11 = (f32[2,16,2,512]{3,1,0,2:T(8,128)S(1)}, f32[2,16,2,512]{3,1,0,2:T(8,128)S(1)}, u32[]{:S(2)}, u32[]{:S(2)}) collective-permute-start(f32[2,16,2,512]{3,1,0,2:T(8,128)S(1)} %fusion.18), channel_id=1, source_target_pairs={{0,64},{4,68},{8,72},{12,76},{16,80},{20,84},{24,88},{28,92},{32,9... | collective-permute-start | bytes 393224 | tf_op jit(solution)/shard_map/ppermute | solution.py:11
  173.6 8.2 %collective-permute-start.25 = (f32[2,17,2,512]{3,1,2,0:T(8,128)S(1)}, f32[2,17,2,512]{3,1,2,0:T(8,128)S(1)}, u32[]{:S(2)}, u32[]{:S(2)}) collective-permute-start(f32[2,17,2,512]{3,1,2,0:T(8,128)S(1)} %fusion.11), channel_id=1, source_target_pairs={{0,64},{4,68},{8,72},{12,76},{16,80},{20,84},{24,88},{28,92},{32,9... | collective-permute-start | bytes 417800 | tf_op jit(solution)/shard_map/ppermute | solution.py:11
  177.0 12.1 %collective-permute-start.12 = (f32[2,16,2,512]{3,1,0,2:T(8,128)S(1)}, f32[2,16,2,512]{3,1,0,2:T(8,128)S(1)}, u32[]{:S(2)}, u32[]{:S(2)}) collective-permute-start(f32[2,16,2,512]{3,1,0,2:T(8,128)S(1)} %fusion.19), channel_id=1, source_target_pairs={{0,128},{4,132},{8,136},{12,140},{16,144},{20,148},{24,152},{28,15... | collective-permute-start | bytes 393224 | tf_op jit(solution)/shard_map/ppermute | solution.py:11
  181.9 15.6 %collective-permute-start.26 = (f32[2,17,2,512]{3,1,2,0:T(8,128)S(1)}, f32[2,17,2,512]{3,1,2,0:T(8,128)S(1)}, u32[]{:S(2)}, u32[]{:S(2)}) collective-permute-start(f32[2,17,2,512]{3,1,2,0:T(8,128)S(1)} %fusion.12), channel_id=1, source_target_pairs={{0,128},{4,132},{8,136},{12,140},{16,144},{20,148},{24,152},{28,15... | collective-permute-start | bytes 417800 | tf_op jit(solution)/shard_map/ppermute | solution.py:11
  189.2 13.1 %collective-permute-start.13 = (f32[2,16,2,512]{3,1,0,2:T(8,128)S(1)}, f32[2,16,2,512]{3,1,0,2:T(8,128)S(1)}, u32[]{:S(2)}, u32[]{:S(2)}) collective-permute-start(f32[2,16,2,512]{3,1,0,2:T(8,128)S(1)} %fusion.20), channel_id=1, source_target_pairs={{0,256},{4,260},{8,264},{12,268},{16,272},{20,276},{24,280},{28,28... | collective-permute-start | bytes 393224 | tf_op jit(solution)/shard_map/ppermute | solution.py:11
  197.6 15.6 %collective-permute-start.27 = (f32[2,17,2,512]{3,1,2,0:T(8,128)S(1)}, f32[2,17,2,512]{3,1,2,0:T(8,128)S(1)}, u32[]{:S(2)}, u32[]{:S(2)}) collective-permute-start(f32[2,17,2,512]{3,1,2,0:T(8,128)S(1)} %fusion.13), channel_id=1, source_target_pairs={{0,256},{4,260},{8,264},{12,268},{16,272},{20,276},{24,280},{28,28... | collective-permute-start | bytes 417800 | tf_op jit(solution)/shard_map/ppermute | solution.py:11
  307.3 0.7 copy-start.5
where the time goes:
time: 618 us; the launch traced here: 617 us
  blocking collectives  400 us (65%)
  starting transfers between devices  115 us (19%)
  waiting for transfers between devices  73.9 us (12%)
  matrix products  11.2 us (2%)
  other arithmetic  7.95 us (1%)
    psum x1, blocking collectives, per_device(): sum_skip = lax.psum(part_skip, 'seq')  307 us
    ppermute x28, starting transfers between devices, partner_2(): lax.ppermute(shard, axis, [(i, i ^ 1 << stride) for i in range(lax.axis_s...  115 us
    psum x1, blocking collectives, per_device(): lax.psum((part_residue, part_memory), ('seq', 'ch'))  93.2 us
    ppermute x28, waiting for transfers between devices, partner_2(): lax.ppermute(shard, axis, [(i, i ^ 1 << stride) for i in range(lax.axis_s...  73.9 us
  transfers between devices with their start and end apart: 28, of which 20 were waited for; matrix products, arithmetic and copies ran while one was open for 1% of the time, Pallas kernels for 0%

commit v1 on v0

--- a/solution.py
+++ b/solution.py
@@ -189,7 +189,7 @@
     part_skip = jnp.sum(grad_mixed * values, axis=1)
     all_channels = channels * lax.axis_size("ch")
     seq_total = devices * local_len
-    sum_residue, sum_memory = lax.psum((part_residue, part_memory), ("seq", "ch"))
+    sum_residue, sum_memory = lax.psum(lax.psum((part_residue, part_memory), "ch"), "seq")
     sum_skip = lax.psum(part_skip, "seq")
     norm_scale = 1.0 / math.sqrt(all_channels * seq_total)
     grad_skip = sum_skip / math.sqrt(seq_total)

time: 618 us -> 531 us (0.86)
  blocking collectives: 400 us -> 314 us
    psum x1, blocking collectives: 93.2 us -> 7.27 us  [per_device(): lax.psum((part_residue, part_memory), 'ch')]
where the time goes in v1:
time: 531 us; the launch traced here: 530 us
  blocking collectives  314 us (59%)
  starting transfers between devices  115 us (22%)
  waiting for transfers between devices  73.9 us (14%)
  matrix products  11.2 us (2%)
  other arithmetic  7.94 us (1%)
    psum x1, blocking collectives, per_device(): sum_skip = lax.psum(part_skip, 'seq')  306 us
    ppermute x28, starting transfers between devices, partner_2(): lax.ppermute(shard, axis, [(i, i ^ 1 << stride) for i in range(lax.axis_s...  115 us
    ppermute x28, waiting for transfers between devices, partner_2(): lax.ppermute(shard, axis, [(i, i ^ 1 << stride) for i in range(lax.axis_s...  73.9 us
  transfers between devices with their start and end apart: 28, of which 20 were waited for; matrix products, arithmetic and copies ran while one was open for 1% of the time, Pallas kernels for 0%

profile of v1, /device:TPU:4, one launch (start us, length us, event | category | flops | bytes accessed | tf_op | source)
XLA Modules:
  0.0 530.1 jit_solution(325985558130426324)
XLA Ops:
  0.8 0.6 copy-done.6
  2.3 7.7 %collective-permute-start = (f32[2,17,2,512]{3,1,2,0:T(8,128)S(1)}, f32[2,17,2,512]{3,1,2,0:T(8,128)S(1)}, u32[]{:S(2)}, u32[]{:S(2)}) collective-permute-start(f32[2,17,2,512]{3,1,2,0:T(8,128)S(1)} %pad_maximum_fusion.13), channel_id=1, source_target_pairs={{0,256},{4,260},{8,264},{12,268},{16,272},{20,276},{24,280},{28,28... | collective-permute-start | bytes 417800 | tf_op jit(solution)/shard_map/ppermute | solution.py:11
  10.1 2.0 collective-permute-start.14
  13.4 10.8 %collective-permute-done.14 = f32[2,16,2,512]{3,1,0,2:T(8,128)S(1)} collective-permute-done((f32[2,16,2,512]{3,1,0,2:T(8,128)S(1)}, f32[2,16,2,512]{3,1,0,2:T(8,128)S(1)}, u32[]{:S(2)}, u32[]{:S(2)}) %collective-permute-start.14) | collective-permute-done | bytes 131104 | tf_op jit(solution)/shard_map/ppermute | solution.py:11
  24.4 4.9 collective-permute-start.15
  29.4 1.9 collective-permute-start.1
  31.4 7.9 %collective-permute-done.15 = f32[2,16,2,512]{3,1,0,2:T(8,128)S(1)} collective-permute-done((f32[2,16,2,512]{3,1,0,2:T(8,128)S(1)}, f32[2,16,2,512]{3,1,0,2:T(8,128)S(1)}, u32[]{:S(2)}, u32[]{:S(2)}) %collective-permute-start.15) | collective-permute-done | bytes 131104 | tf_op jit(solution)/shard_map/ppermute | solution.py:11
  39.4 1.9 collective-permute-start.16
  41.3 1.8 collective-permute-done.1
  43.3 2.1 collective-permute-start.2
  45.5 0.8 collective-permute-done.16
  46.3 3.1 collective-permute-start.17
  49.4 2.4 collective-permute-done.2
  51.9 3.1 collective-permute-start.3
  55.1 10.9 %collective-permute-start.18 = (f32[2,16,2,512]{3,1,0,2:T(8,128)S(1)}, f32[2,16,2,512]{3,1,0,2:T(8,128)S(1)}, u32[]{:S(2)}, u32[]{:S(2)}) collective-permute-start(f32[2,16,2,512]{3,1,0,2:T(8,128)S(1)} %maximum_select_fusion.10), channel_id=1, source_target_pairs={{0,16},{4,20},{8,24},{12,28},{16,0},{20,4},{24,8},{28,12},{32,48},... | collective-permute-start | bytes 393224 | tf_op jit(solution)/shard_map/ppermute | solution.py:11
  66.2 4.3 collective-permute-start.4
  70.8 7.4 %collective-permute-start.19 = (f32[2,16,2,512]{3,1,0,2:T(8,128)S(1)}, f32[2,16,2,512]{3,1,0,2:T(8,128)S(1)}, u32[]{:S(2)}, u32[]{:S(2)}) collective-permute-start(f32[2,16,2,512]{3,1,0,2:T(8,128)S(1)} %maximum_select_fusion.11), channel_id=1, source_target_pairs={{0,8},{4,12},{8,0},{12,4},{16,24},{20,28},{24,16},{28,20},{32,40},... | collective-permute-start | bytes 393224 | tf_op jit(solution)/shard_map/ppermute | solution.py:11
  78.2 3.5 collective-permute-done.4
  81.8 4.0 collective-permute-start.5
  85.8 3.4 collective-permute-done.19
  89.3 2.0 collective-permute-start.20
  91.3 4.3 collective-permute-done.5
  95.7 2.1 collective-permute-start.6
  98.9 0.6 convolution_bitcast_fusion.4
  99.5 0.6 convolution_bitcast_fusion.5
  100.1 4.2 collective-permute-done.6
  105.0 0.6 convolution_bitcast_fusion.2
  105.6 0.6 convolution_bitcast_fusion.3
  106.4 1.1 fusion
  107.5 1.1 fusion.2
  109.6 0.6 fusion.46
  110.2 0.6 fusion.52
  111.1 0.6 fusion.4
  111.7 0.6 fusion.5
  112.4 0.6 copy-done.4
  114.1 0.7 fusion.7
  114.8 0.7 fusion.6
  115.6 0.9 convolution_bitcast_fusion.1
  116.5 0.6 convolution_bitcast_fusion
  118.9 2.2 collective-permute-start.21
  121.6 3.6 collective-permute-start.7
  125.2 4.2 collective-permute-done.7
  129.5 2.8 collective-permute-start.8
  132.5 3.9 collective-permute-start.22
  136.4 9.4 %collective-permute-done.8 = f32[2,16,2,512]{3,1,0,2:T(8,128)S(1)} collective-permute-done((f32[2,16,2,512]{3,1,0,2:T(8,128)S(1)}, f32[2,16,2,512]{3,1,0,2:T(8,128)S(1)}, u32[]{:S(2)}, u32[]{:S(2)}) %collective-permute-start.8) | collective-permute-done | bytes 131104 | tf_op jit(solution)/shard_map/ppermute | solution.py:11
  145.9 4.5 collective-permute-start.9
  150.6 5.6 %collective-permute-start.23 = (f32[2,17,2,512]{3,1,2,0:T(8,128)S(1)}, f32[2,17,2,512]{3,1,2,0:T(8,128)S(1)}, u32[]{:S(2)}, u32[]{:S(2)}) collective-permute-start(f32[2,17,2,512]{3,1,2,0:T(8,128)S(1)} %fusion.9), channel_id=1, source_target_pairs={{0,16},{4,20},{8,24},{12,28},{16,0},{20,4},{24,8},{28,12},{32,48},... | collective-permute-start | bytes 417800 | tf_op jit(solution)/shard_map/ppermute | solution.py:11
  156.3 1.6 collective-permute-done.9
  157.9 7.1 %collective-permute-start.10 = (f32[2,16,2,512]{3,1,0,2:T(8,128)S(1)}, f32[2,16,2,512]{3,1,0,2:T(8,128)S(1)}, u32[]{:S(2)}, u32[]{:S(2)}) collective-permute-start(f32[2,16,2,512]{3,1,0,2:T(8,128)S(1)} %fusion.17), channel_id=1, source_target_pairs={{0,32},{4,36},{8,40},{12,44},{16,48},{20,52},{24,56},{28,60},{32,0... | collective-permute-start | bytes 393224 | tf_op jit(solution)/shard_map/ppermute | solution.py:11
  165.1 0.7 collective-permute-done.23
  165.9 3.3 collective-permute-start.24
  169.3 3.7 collective-permute-start.11
  173.6 3.3 collective-permute-start.25
  177.0 4.4 collective-permute-start.12
  181.9 4.4 collective-permute-start.26
  186.4 2.8 collective-permute-done.12
  189.2 4.3 collective-permute-start.13
  193.5 4.0 collective-permute-done.26
  197.6 4.7 collective-permute-start.27
  202.5 10.7 %collective-permute-done.27 = f32[2,17,2,512]{3,1,2,0:T(8,128)S(1)} collective-permute-done((f32[2,17,2,512]{3,1,2,0:T(8,128)S(1)}, f32[2,17,2,512]{3,1,2,0:T(8,128)S(1)}, u32[]{:S(2)}, u32[]{:S(2)}) %collective-permute-start.27) | collective-permute-done | bytes 139296 | tf_op jit(solution)/shard_map/ppermute | solution.py:11
  213.6 7.3 %all-reduce.4 = (f32[16]{0:T(128)S(1)}, f32[16]{0:T(128)S(1)}) all-reduce(f32[16]{0:T(128)S(1)} %get-tuple-element.8, f32[16]{0:T(128)S(1)} %mul.2458), channel_id=1, replica_groups=mesh['seq'=128,'ch'=4] {'ch'}, use_global_device_ids=true, to_apply=%region_5.6 | all-reduce | flops 32 | bytes 256 | tf_op jit(solution)/shard_map/psum | solution.py:192
  220.9 0.8 fusion.29
  221.7 306.3 %all-reduce.3 = (f32[16]{0:T(128)S(1)}, f32[16]{0:T(128)S(1)}, f32[16]{0:T(128)S(1)}) all-reduce(f32[16]{0:T(128)S(1)} %get-tuple-element.133, f32[16]{0:T(128)S(1)} %get-tuple-element.12, f32[16]{0:T(128)S(1)} %get-tuple-element.13), channel_id=1, replica_groups=mesh['seq'=128,'ch'=4] {'seq'}, use_global_device_ids=true, to_apply=%region_3.4 | all-reduce | flops 48 | bytes 384 | tf_op jit(solution)/shard_map/psum | solution.py:193
  529.5 0.6 fusion.28
  (195 shorter events, 12.8 us)
Async XLA Ops:
  0.8 0.7 copy-start.6
  0.8 0.7 copy-start.7
  1.4 0.7 copy-start.2
  1.5 0.7 copy-start.1
  2.3 7.8 %copy-start = (bf16[16,512]{1,0:T(8,128)(2,1)S(1)}, bf16[16,512]{1,0:T(8,128)(2,1)}, u32[]{:S(2)}) copy-start(bf16[16,512]{1,0:T(8,128)(2,1)} %param.9) | copy-start | bytes 49156
  2.3 7.8 %copy-start.3 = (bf16[16,512]{1,0:T(8,128)(2,1)S(1)}, bf16[16,512]{1,0:T(8,128)(2,1)}, u32[]{:S(2)}) copy-start(bf16[16,512]{1,0:T(8,128)(2,1)} %param.14) | copy-start | bytes 49156
  2.3 27.0 %collective-permute-start = (f32[2,17,2,512]{3,1,2,0:T(8,128)S(1)}, f32[2,17,2,512]{3,1,2,0:T(8,128)S(1)}, u32[]{:S(2)}, u32[]{:S(2)}) collective-permute-start(f32[2,17,2,512]{3,1,2,0:T(8,128)S(1)} %pad_maximum_fusion.13), channel_id=1, source_target_pairs={{0,256},{4,260},{8,264},{12,268},{16,272},{20,276},{24,280},{28,28... | collective-permute-start | bytes 417800 | tf_op jit(solution)/shard_map/ppermute | solution.py:11
  10.1 14.1 %collective-permute-start.14 = (f32[2,16,2,512]{3,1,0,2:T(8,128)S(1)}, f32[2,16,2,512]{3,1,0,2:T(8,128)S(1)}, u32[]{:S(2)}, u32[]{:S(2)}) collective-permute-start(f32[2,16,2,512]{3,1,0,2:T(8,128)S(1)} %pad_maximum_fusion.16), channel_id=1, source_target_pairs={{0,256},{4,260},{8,264},{12,268},{16,272},{20,276},{24,280},{28,28... | collective-permute-start | bytes 393224 | tf_op jit(solution)/shard_map/ppermute | solution.py:11
  24.4 14.9 %collective-permute-start.15 = (f32[2,16,2,512]{3,1,0,2:T(8,128)S(1)}, f32[2,16,2,512]{3,1,0,2:T(8,128)S(1)}, u32[]{:S(2)}, u32[]{:S(2)}) collective-permute-start(f32[2,16,2,512]{3,1,0,2:T(8,128)S(1)} %maximum_select_fusion.7), channel_id=1, source_target_pairs={{0,128},{4,132},{8,136},{12,140},{16,144},{20,148},{24,152},{28,15... | collective-permute-start | bytes 393224 | tf_op jit(solution)/shard_map/ppermute | solution.py:11
  29.4 13.7 %collective-permute-start.1 = (f32[2,17,2,512]{3,1,2,0:T(8,128)S(1)}, f32[2,17,2,512]{3,1,2,0:T(8,128)S(1)}, u32[]{:S(2)}, u32[]{:S(2)}) collective-permute-start(f32[2,17,2,512]{3,1,2,0:T(8,128)S(1)} %maximum_select_fusion), channel_id=1, source_target_pairs={{0,128},{4,132},{8,136},{12,140},{16,144},{20,148},{24,152},{28,15... | collective-permute-start | bytes 417800 | tf_op jit(solution)/shard_map/ppermute | solution.py:11
  39.4 6.9 %collective-permute-start.16 = (f32[2,16,2,512]{3,1,0,2:T(8,128)S(1)}, f32[2,16,2,512]{3,1,0,2:T(8,128)S(1)}, u32[]{:S(2)}, u32[]{:S(2)}) collective-permute-start(f32[2,16,2,512]{3,1,0,2:T(8,128)S(1)} %maximum_select_fusion.8), channel_id=1, source_target_pairs={{0,64},{4,68},{8,72},{12,76},{16,80},{20,84},{24,88},{28,92},{32,9... | collective-permute-start | bytes 393224 | tf_op jit(solution)/shard_map/ppermute | solution.py:11
  43.3 8.5 %collective-permute-start.2 = (f32[2,17,2,512]{3,1,2,0:T(8,128)S(1)}, f32[2,17,2,512]{3,1,2,0:T(8,128)S(1)}, u32[]{:S(2)}, u32[]{:S(2)}) collective-permute-start(f32[2,17,2,512]{3,1,2,0:T(8,128)S(1)} %maximum_select_fusion.1), channel_id=1, source_target_pairs={{0,64},{4,68},{8,72},{12,76},{16,80},{20,84},{24,88},{28,92},{32,9... | collective-permute-start | bytes 417800 | tf_op jit(solution)/shard_map/ppermute | solution.py:11
  46.3 8.7 %collective-permute-start.17 = (f32[2,16,2,512]{3,1,0,2:T(8,128)S(1)}, f32[2,16,2,512]{3,1,0,2:T(8,128)S(1)}, u32[]{:S(2)}, u32[]{:S(2)}) collective-permute-start(f32[2,16,2,512]{3,1,0,2:T(8,128)S(1)} %maximum_select_fusion.9), channel_id=1, source_target_pairs={{0,32},{4,36},{8,40},{12,44},{16,48},{20,52},{24,56},{28,60},{32,0... | collective-permute-start | bytes 393224 | tf_op jit(solution)/shard_map/ppermute | solution.py:11
  51.9 14.1 %collective-permute-start.3 = (f32[2,17,2,512]{3,1,2,0:T(8,128)S(1)}, f32[2,17,2,512]{3,1,2,0:T(8,128)S(1)}, u32[]{:S(2)}, u32[]{:S(2)}) collective-permute-start(f32[2,17,2,512]{3,1,2,0:T(8,128)S(1)} %maximum_select_fusion.2), channel_id=1, source_target_pairs={{0,32},{4,36},{8,40},{12,44},{16,48},{20,52},{24,56},{28,60},{32,0... | collective-permute-start | bytes 417800 | tf_op jit(solution)/shard_map/ppermute | solution.py:11
  55.1 15.6 %collective-permute-start.18 = (f32[2,16,2,512]{3,1,0,2:T(8,128)S(1)}, f32[2,16,2,512]{3,1,0,2:T(8,128)S(1)}, u32[]{:S(2)}, u32[]{:S(2)}) collective-permute-start(f32[2,16,2,512]{3,1,0,2:T(8,128)S(1)} %maximum_select_fusion.10), channel_id=1, source_target_pairs={{0,16},{4,20},{8,24},{12,28},{16,0},{20,4},{24,8},{28,12},{32,48},... | collective-permute-start | bytes 393224 | tf_op jit(solution)/shard_map/ppermute | solution.py:11
  66.2 15.5 %collective-permute-start.4 = (f32[2,17,2,512]{3,1,2,0:T(8,128)S(1)}, f32[2,17,2,512]{3,1,2,0:T(8,128)S(1)}, u32[]{:S(2)}, u32[]{:S(2)}) collective-permute-start(f32[2,17,2,512]{3,1,2,0:T(8,128)S(1)} %maximum_select_fusion.3), channel_id=1, source_target_pairs={{0,16},{4,20},{8,24},{12,28},{16,0},{20,4},{24,8},{28,12},{32,48},... | collective-permute-start | bytes 417800 | tf_op jit(solution)/shard_map/ppermute | solution.py:11
  70.8 18.4 %collective-permute-start.19 = (f32[2,16,2,512]{3,1,0,2:T(8,128)S(1)}, f32[2,16,2,512]{3,1,0,2:T(8,128)S(1)}, u32[]{:S(2)}, u32[]{:S(2)}) collective-permute-start(f32[2,16,2,512]{3,1,0,2:T(8,128)S(1)} %maximum_select_fusion.11), channel_id=1, source_target_pairs={{0,8},{4,12},{8,0},{12,4},{16,24},{20,28},{24,16},{28,20},{32,40},... | collective-permute-start | bytes 393224 | tf_op jit(solution)/shard_map/ppermute | solution.py:11
  81.8 13.8 %collective-permute-start.5 = (f32[2,17,2,512]{3,1,2,0:T(8,128)S(1)}, f32[2,17,2,512]{3,1,2,0:T(8,128)S(1)}, u32[]{:S(2)}, u32[]{:S(2)}) collective-permute-start(f32[2,17,2,512]{3,1,2,0:T(8,128)S(1)} %maximum_select_fusion.4), channel_id=1, source_target_pairs={{0,8},{4,12},{8,0},{12,4},{16,24},{20,28},{24,16},{28,20},{32,40},... | collective-permute-start | bytes 417800 | tf_op jit(solution)/shard_map/ppermute | solution.py:11
  89.3 8.9 %collective-permute-start.20 = (f32[2,16,2,512]{3,1,0,2:T(8,128)S(1)}, f32[2,16,2,512]{3,1,0,2:T(8,128)S(1)}, u32[]{:S(2)}, u32[]{:S(2)}) collective-permute-start(f32[2,16,2,512]{3,1,0,2:T(8,128)S(1)} %maximum_select_fusion.12), channel_id=1, source_target_pairs={{0,4},{4,0},{8,12},{12,8},{16,20},{20,16},{24,28},{28,24},{32,36},... | collective-permute-start | bytes 393224 | tf_op jit(solution)/shard_map/ppermute | solution.py:11
  95.7 8.6 %collective-permute-start.6 = (f32[2,17,2,512]{3,1,2,0:T(8,128)S(1)}, f32[2,17,2,512]{3,1,2,0:T(8,128)S(1)}, u32[]{:S(2)}, u32[]{:S(2)}) collective-permute-start(f32[2,17,2,512]{3,1,2,0:T(8,128)S(1)} %maximum_select_fusion.5), channel_id=1, source_target_pairs={{0,4},{4,0},{8,12},{12,8},{16,20},{20,16},{24,28},{28,24},{32,36},... | collective-permute-start | bytes 417800 | tf_op jit(solution)/shard_map/ppermute | solution.py:11
  112.4 0.7 copy-start.4
  118.9 13.5 %collective-permute-start.21 = (f32[2,17,2,512]{3,1,2,0:T(8,128)S(1)}, f32[2,17,2,512]{3,1,2,0:T(8,128)S(1)}, u32[]{:S(2)}, u32[]{:S(2)}) collective-permute-start(f32[2,17,2,512]{3,1,2,0:T(8,128)S(1)} %pad_maximum_fusion.14), channel_id=1, source_target_pairs={{0,4},{4,0},{8,12},{12,8},{16,20},{20,16},{24,28},{28,24},{32,36},... | collective-permute-start | bytes 417800 | tf_op jit(solution)/shard_map/ppermute | solution.py:11
  121.6 7.9 %collective-permute-start.7 = (f32[2,16,2,512]{3,1,0,2:T(8,128)S(1)}, f32[2,16,2,512]{3,1,0,2:T(8,128)S(1)}, u32[]{:S(2)}, u32[]{:S(2)}) collective-permute-start(f32[2,16,2,512]{3,1,0,2:T(8,128)S(1)} %pad_maximum_fusion.15), channel_id=1, source_target_pairs={{0,4},{4,0},{8,12},{12,8},{16,20},{20,16},{24,28},{28,24},{32,36},... | collective-permute-start | bytes 393224 | tf_op jit(solution)/shard_map/ppermute | solution.py:11
  129.5 16.3 %collective-permute-start.8 = (f32[2,16,2,512]{3,1,0,2:T(8,128)S(1)}, f32[2,16,2,512]{3,1,0,2:T(8,128)S(1)}, u32[]{:S(2)}, u32[]{:S(2)}) collective-permute-start(f32[2,16,2,512]{3,1,0,2:T(8,128)S(1)} %fusion.15), channel_id=1, source_target_pairs={{0,8},{4,12},{8,0},{12,4},{16,24},{20,28},{24,16},{28,20},{32,40},... | collective-permute-start | bytes 393224 | tf_op jit(solution)/shard_map/ppermute | solution.py:11
  132.5 17.9 %collective-permute-start.22 = (f32[2,17,2,512]{3,1,2,0:T(8,128)S(1)}, f32[2,17,2,512]{3,1,2,0:T(8,128)S(1)}, u32[]{:S(2)}, u32[]{:S(2)}) collective-permute-start(f32[2,17,2,512]{3,1,2,0:T(8,128)S(1)} %fusion.8), channel_id=1, source_target_pairs={{0,8},{4,12},{8,0},{12,4},{16,24},{20,28},{24,16},{28,20},{32,40},... | collective-permute-start | bytes 417800 | tf_op jit(solution)/shard_map/ppermute | solution.py:11
  145.9 11.9 %collective-permute-start.9 = (f32[2,16,2,512]{3,1,0,2:T(8,128)S(1)}, f32[2,16,2,512]{3,1,0,2:T(8,128)S(1)}, u32[]{:S(2)}, u32[]{:S(2)}) collective-permute-start(f32[2,16,2,512]{3,1,0,2:T(8,128)S(1)} %fusion.16), channel_id=1, source_target_pairs={{0,16},{4,20},{8,24},{12,28},{16,0},{20,4},{24,8},{28,12},{32,48},... | collective-permute-start | bytes 393224 | tf_op jit(solution)/shard_map/ppermute | solution.py:11
  150.6 15.2 %collective-permute-start.23 = (f32[2,17,2,512]{3,1,2,0:T(8,128)S(1)}, f32[2,17,2,512]{3,1,2,0:T(8,128)S(1)}, u32[]{:S(2)}, u32[]{:S(2)}) collective-permute-start(f32[2,17,2,512]{3,1,2,0:T(8,128)S(1)} %fusion.9), channel_id=1, source_target_pairs={{0,16},{4,20},{8,24},{12,28},{16,0},{20,4},{24,8},{28,12},{32,48},... | collective-permute-start | bytes 417800 | tf_op jit(solution)/shard_map/ppermute | solution.py:11
  157.9 11.3 %collective-permute-start.10 = (f32[2,16,2,512]{3,1,0,2:T(8,128)S(1)}, f32[2,16,2,512]{3,1,0,2:T(8,128)S(1)}, u32[]{:S(2)}, u32[]{:S(2)}) collective-permute-start(f32[2,16,2,512]{3,1,0,2:T(8,128)S(1)} %fusion.17), channel_id=1, source_target_pairs={{0,32},{4,36},{8,40},{12,44},{16,48},{20,52},{24,56},{28,60},{32,0... | collective-permute-start | bytes 393224 | tf_op jit(solution)/shard_map/ppermute | solution.py:11
  165.9 7.6 %collective-permute-start.24 = (f32[2,17,2,512]{3,1,2,0:T(8,128)S(1)}, f32[2,17,2,512]{3,1,2,0:T(8,128)S(1)}, u32[]{:S(2)}, u32[]{:S(2)}) collective-permute-start(f32[2,17,2,512]{3,1,2,0:T(8,128)S(1)} %fusion.10), channel_id=1, source_target_pairs={{0,32},{4,36},{8,40},{12,44},{16,48},{20,52},{24,56},{28,60},{32,0... | collective-permute-start | bytes 417800 | tf_op jit(solution)/shard_map/ppermute | solution.py:11
  169.3 7.6 %collective-permute-start.11 = (f32[2,16,2,512]{3,1,0,2:T(8,128)S(1)}, f32[2,16,2,512]{3,1,0,2:T(8,128)S(1)}, u32[]{:S(2)}, u32[]{:S(2)}) collective-permute-start(f32[2,16,2,512]{3,1,0,2:T(8,128)S(1)} %fusion.18), channel_id=1, source_target_pairs={{0,64},{4,68},{8,72},{12,76},{16,80},{20,84},{24,88},{28,92},{32,9... | collective-permute-start | bytes 393224 | tf_op jit(solution)/shard_map/ppermute | solution.py:11
  173.6 8.2 %collective-permute-start.25 = (f32[2,17,2,512]{3,1,2,0:T(8,128)S(1)}, f32[2,17,2,512]{3,1,2,0:T(8,128)S(1)}, u32[]{:S(2)}, u32[]{:S(2)}) collective-permute-start(f32[2,17,2,512]{3,1,2,0:T(8,128)S(1)} %fusion.11), channel_id=1, source_target_pairs={{0,64},{4,68},{8,72},{12,76},{16,80},{20,84},{24,88},{28,92},{32,9... | collective-permute-start | bytes 417800 | tf_op jit(solution)/shard_map/ppermute | solution.py:11
  177.0 12.1 %collective-permute-start.12 = (f32[2,16,2,512]{3,1,0,2:T(8,128)S(1)}, f32[2,16,2,512]{3,1,0,2:T(8,128)S(1)}, u32[]{:S(2)}, u32[]{:S(2)}) collective-permute-start(f32[2,16,2,512]{3,1,0,2:T(8,128)S(1)} %fusion.19), channel_id=1, source_target_pairs={{0,128},{4,132},{8,136},{12,140},{16,144},{20,148},{24,152},{28,15... | collective-permute-start | bytes 393224 | tf_op jit(solution)/shard_map/ppermute | solution.py:11
  181.9 15.6 %collective-permute-start.26 = (f32[2,17,2,512]{3,1,2,0:T(8,128)S(1)}, f32[2,17,2,512]{3,1,2,0:T(8,128)S(1)}, u32[]{:S(2)}, u32[]{:S(2)}) collective-permute-start(f32[2,17,2,512]{3,1,2,0:T(8,128)S(1)} %fusion.12), channel_id=1, source_target_pairs={{0,128},{4,132},{8,136},{12,140},{16,144},{20,148},{24,152},{28,15... | collective-permute-start | bytes 417800 | tf_op jit(solution)/shard_map/ppermute | solution.py:11
  189.2 13.1 %collective-permute-start.13 = (f32[2,16,2,512]{3,1,0,2:T(8,128)S(1)}, f32[2,16,2,512]{3,1,0,2:T(8,128)S(1)}, u32[]{:S(2)}, u32[]{:S(2)}) collective-permute-start(f32[2,16,2,512]{3,1,0,2:T(8,128)S(1)} %fusion.20), channel_id=1, source_target_pairs={{0,256},{4,260},{8,264},{12,268},{16,272},{20,276},{24,280},{28,28... | collective-permute-start | bytes 393224 | tf_op jit(solution)/shard_map/ppermute | solution.py:11
  197.6 15.6 %collective-permute-start.27 = (f32[2,17,2,512]{3,1,2,0:T(8,128)S(1)}, f32[2,17,2,512]{3,1,2,0:T(8,128)S(1)}, u32[]{:S(2)}, u32[]{:S(2)}) collective-permute-start(f32[2,17,2,512]{3,1,2,0:T(8,128)S(1)} %fusion.13), channel_id=1, source_target_pairs={{0,256},{4,260},{8,264},{12,268},{16,272},{20,276},{24,280},{28,28... | collective-permute-start | bytes 417800 | tf_op jit(solution)/shard_map/ppermute | solution.py:11
  213.6 7.3 %copy-start.5 = (f32[16]{0:T(128)S(1)}, f32[16]{0:T(128)}, u32[]{:S(2)}) copy-start(f32[16]{0:T(128)} %param.11) | copy-start | bytes 196
